TPU v7x, 128 devices: a whole 4x4x4 slice. The times are simulated.
128 devices in a mesh: grp: 8 (over y, core), dom: 16 (over z, x).
Axes of the slice: x: 4, y: 4, z: 4, core: 2. Of those that a mesh axis runs over, the one named last changes fastest.
Arguments:
- diag_blocks: bfloat16 [2048, 384, 384], P(('grp', 'dom')), may hold values from -0.3125 to 0.3125
- face_in: bfloat16 [4096, 384, 384], P(('grp', 'dom')), may hold values from -0.3125 to 0.3125
- face_cross: bfloat16 [2048, 384, 384], P(('grp', 'dom')), may hold values from -0.3125 to 0.3125
- metric: float32 [2048, 384], P(('grp', 'dom')), may hold values from 0.5 to 2
- source_in: int32 [4096], P(('grp', 'dom')), may hold values from 0 to 15
- source_cross: int32 [2048], P(('grp', 'dom')), may hold values from 0 to 15
- orient_in: int32 [4096], P(('grp', 'dom')), may hold values from 0 to 7
- orient_cross: int32 [2048], P(('grp', 'dom')), may hold values from 0 to 7
- peer_in: int32 [4096, 1], P(('grp', 'dom')), may hold values from 0 to 15; in each aligned block of 32 rows (0 to 31, 32 to 63, ...) at most 3 rows name the same one
- peer_cross: int32 [2048, 1], P(('grp', 'dom')), may hold values from 0 to 7; in each aligned block of 16 rows (0 to 15, 16 to 31, ...) at most 3 rows name the same one
- target_in: int32 [4096], P(('grp', 'dom')), may hold values from 0 to 47
- target_cross: int32 [2048], P(('grp', 'dom')), may hold values from 0 to 47
Outputs:
- coarse_diag: float32 [2048, 2304], P('grp')
- coarse_face: float32 [2048, 6912], P('grp')
Inputs may be any that keep to these rules, and one draw needn't show every extreme that they name: `peer_in`: at most 3 records of one device name the same partition; on some device exactly 3 do. `peer_cross`: at most 3 records of one device name the same group; on some device exactly 3 do.
All inputs are finite; a program needn't handle non-finite values.
Results may differ from a plain program's by a relative error of at most 0.0052.
Values may be sent and summed in bfloat16 or wider, within the bound.
A program may use at most 128 MiB of HBM per device.

v0:
```python
import jax
import jax.numpy as jnp
from jax import lax
from jax.sharding import PartitionSpec as P

CROSS_CAP = 3


def corner_table(var_count):
    nodes = -1.0 + 2.0 * jnp.arange(4, dtype=jnp.float32) / 3.0
    basis = jnp.stack(((1.0 - nodes) / 2.0, (1.0 + nodes) / 2.0), axis=1)
    cube = jnp.einsum("ia,jb,kc->abcijk", basis, basis, basis).reshape(8, 64)
    return jnp.kron(jnp.eye(var_count, dtype=jnp.float32), cube)


def restrictor(weights, orient):
    var_count = weights.shape[1] // 64
    table = corner_table(var_count)
    full = weights[:, None, :] * table[None]
    shaped = full.reshape(weights.shape[0], var_count * 8, var_count, 4, 4, 4)
    bits = orient.reshape(-1, 1, 1, 1, 1, 1)
    shaped = jnp.where(bits % 2 == 1, jnp.flip(shaped, 3), shaped)
    shaped = jnp.where(bits // 2 % 2 == 1, jnp.flip(shaped, 4), shaped)
    shaped = jnp.where(bits // 4 % 2 == 1, jnp.flip(shaped, 5), shaped)
    return shaped.reshape(weights.shape[0], var_count * 8, var_count * 64).astype(jnp.bfloat16)


def plain_restrictor(weights):
    table = corner_table(weights.shape[1] // 64)
    return (weights[:, None, :] * table[None]).astype(jnp.bfloat16)


def pick_rows(index, table):
    picks = (index[:, None] == jnp.arange(table.shape[0], dtype=jnp.int32)[None, :]).astype(
        jnp.float32
    )
    return jnp.dot(picks, table, precision=lax.Precision.HIGHEST)


def one_sided(blocks, column_side):
    return jnp.einsum(
        "rcj,rij->rci", column_side, blocks, preferred_element_type=jnp.float32
    ).astype(jnp.bfloat16)


def coarse_terms(row_side, products):
    return jnp.einsum("rci,rdi->rcd", row_side, products, preferred_element_type=jnp.float32)


def id_row(values, width):
    flat = values.reshape(-1).astype(jnp.bfloat16)
    return jnp.pad(flat, (0, width - flat.shape[0]))[None, :]


def per_device(
    diag_blocks,
    face_in,
    face_cross,
    metric,
    source_in,
    source_cross,
    orient_in,
    orient_cross,
    peer_in,
    peer_cross,
    target_in,
    target_cross,
):
    elem_count = metric.shape[0]
    coarse_width = metric.shape[1] // 8
    square = coarse_width * coarse_width
    slots_dev = 3 * elem_count
    group_width = lax.axis_size("dom")
    group_count = lax.axis_size("grp")
    my_dom = lax.axis_index("dom")
    my_grp = lax.axis_index("grp")
    inner_count = face_in.shape[0]
    cross_count = face_cross.shape[0]
    metric_dom = lax.all_gather(metric, "dom", axis=0, tiled=True)
    metric_grp = lax.all_gather(metric, "grp", axis=0, tiled=True)
    diag_side = plain_restrictor(metric)
    diag_c = coarse_terms(diag_side, one_sided(diag_blocks, diag_side))
    diag_rows = diag_c.reshape(elem_count, square).astype(jnp.bfloat16)
    diag_all = lax.all_gather(diag_rows, "dom", axis=0, tiled=True)
    cross_y = one_sided(face_cross, restrictor(pick_rows(source_cross, metric), orient_cross))
    peer_x = peer_cross[:, 0]
    cross_row_side = plain_restrictor(
        pick_rows(peer_x * elem_count + target_cross // 3, metric_grp)
    )
    cross_c = coarse_terms(cross_row_side, cross_y).reshape(cross_count, square)
    cross_ids = jnp.stack((peer_x, target_cross), axis=1)
    cross_packet = jnp.concatenate(
        (cross_c.astype(jnp.bfloat16), id_row(cross_ids, square)), axis=0
    )
    cross_got = lax.all_gather(cross_packet, "grp", axis=0)
    got_rows = cross_got[:, :cross_count, :]
    got_ids = cross_got[:, cross_count, : 2 * cross_count].astype(jnp.int32)
    got_peer = got_ids[:, 0::2]
    got_target = got_ids[:, 1::2]
    match = got_peer == my_grp
    rank = jnp.cumsum(match.astype(jnp.int32), axis=1) - 1
    picks = match[:, None, :] & (
        rank[:, None, :] == jnp.arange(CROSS_CAP, dtype=jnp.int32)[None, :, None]
    )
    mine_rows = (
        jnp.einsum(
            "skr,srq->skq", picks.astype(jnp.bfloat16), got_rows, preferred_element_type=jnp.float32
        )
        .astype(jnp.bfloat16)
        .reshape(group_count * CROSS_CAP, square)
    )
    mine_target = jnp.sum(jnp.where(picks, got_target[:, None, :], 0), axis=2)
    mine_slot = jnp.where(jnp.any(picks, axis=2), my_dom * slots_dev + mine_target, -1).reshape(-1)
    inner_y = one_sided(face_in, restrictor(pick_rows(source_in, metric), orient_in))
    peer_i = peer_in[:, 0]
    inner_row_side = plain_restrictor(pick_rows(peer_i * elem_count + target_in // 3, metric_dom))
    inner_c = coarse_terms(inner_row_side, inner_y).reshape(inner_count, square)
    inner_slot = peer_i * slots_dev + target_in
    slots = jnp.concatenate((inner_slot, mine_slot), axis=0)
    valid = slots >= 0
    slot_code = jnp.stack(
        (jnp.where(valid, slots // 32, -1), jnp.where(valid, slots % 32, 0)), axis=1
    )
    face_packet = jnp.concatenate(
        (inner_c.astype(jnp.bfloat16), mine_rows, id_row(slot_code, square)), axis=0
    )
    face_all = lax.all_gather(face_packet, "dom", axis=0)
    contrib_count = slots.shape[0]
    contrib = face_all[:, :contrib_count, :].reshape(group_width * contrib_count, square)
    codes = face_all[:, contrib_count, : 2 * contrib_count].astype(jnp.int32)
    hi = codes[:, 0::2].reshape(-1)
    lo = codes[:, 1::2].reshape(-1)
    got_slot = jnp.where(hi >= 0, hi * 32 + lo, -1)
    group_slots = group_width * slots_dev
    onehot = (jnp.arange(group_slots, dtype=jnp.int32)[:, None] == got_slot[None, :]).astype(
        jnp.bfloat16
    )
    face = jnp.dot(onehot, contrib, preferred_element_type=jnp.float32)
    coarse_diag = diag_all.astype(jnp.float32)
    coarse_face = face.reshape(group_width * elem_count, 3 * square)
    return (coarse_diag, coarse_face)


def solution(mesh):
    placed = (
        P(("grp", "dom"), None, None),
        P(("grp", "dom"), None, None),
        P(("grp", "dom"), None, None),
        P(("grp", "dom"), None),
        P(("grp", "dom")),
        P(("grp", "dom")),
        P(("grp", "dom")),
        P(("grp", "dom")),
        P(("grp", "dom"), None),
        P(("grp", "dom"), None),
        P(("grp", "dom")),
        P(("grp", "dom")),
    )
    return jax.shard_map(
        per_device,
        mesh=mesh,
        in_specs=placed,
        out_specs=(P("grp", None), P("grp", None)),
        check_vma=False,
    )
```

profile of v0, /device:TPU:1, one launch (start us, length us, event | category | flops | bytes accessed | tf_op | source)
XLA Modules:
  0.0 171.8 jit_solution(11630039760645675383)
XLA Ops:
  7.8 4.3 %fusion.26 = bf16[16,48,48]{2,1,0:T(8,128)(2,1)S(1)} fusion(bf16[16,384,384]{2,1,0:T(8,128)(2,1)} %param.12, f32[48,384]{1,0:T(8,128)S(1)} %mul.191, f32[16,384]{1,0:T(8,128)} %param.15), kind=kOutput, calls=%fused_computation.30 | convolution fusion | flops 256315392 | bytes 4890624 | tf_op jit(solution)/shard_map/rci,rdi->rcd/dot_general | solution.py:47
  12.0 0.9 convert_element_type.104
  13.2 14.6 %all_gather.23 = f32[128,384]{1,0:T(8,128)S(1)} all-gather(f32[16,384]{1,0:T(8,128)S(1)} %copy-done), channel_id=1, replica_groups=mesh['grp'=8,'dom'=16] {'grp'}, dimensions={0}, use_global_device_ids=true | all-gather | bytes 221184 | tf_op jit(solution)/shard_map/all_gather | solution.py:80
  28.1 0.4 fusion.43
  28.6 1.0 broadcast_multiply_fusion.1
  29.6 0.6 reverse_select_fusion.5
  30.2 0.7 reverse_select_fusion.4
  30.9 0.7 fusion.1
  31.6 0.2 fusion.42
  31.8 4.3 %fusion.27 = bf16[16,48,48]{2,1,0:T(8,128)(2,1)S(1)} fusion(bf16[16,384,384]{2,1,0:T(8,128)(2,1)} %param.14, bf16[16,48,384]{1,0,2:T(8,128)(2,1)S(1)} %bitcast.38, f32[16,384]{1,0:T(8,128)S(1)} %fusion.42, f32[48,384]{1,0:T(8,128)S(1)} %mul.191), kind=kOutput, calls=%fused_computation.31 | convolution fusion | flops 255725568 | bytes 5480448 | tf_op jit(solution)/shard_map/rci,rdi->rcd/dot_general | solution.py:47
  36.1 0.2 convert_element_type.117
  36.6 13.5 %all-gather.2 = bf16[8,17,2304]{2,1,0:T(8,128)(2,1)S(1)} all-gather(bf16[1,17,2304]{2,1,0:T(8,128)(2,1)S(1)} %maximum_bitcast_fusion.1), channel_id=2, replica_groups=mesh['grp'=8,'dom'=16] {'grp'}, dimensions={0}, use_global_device_ids=true | all-gather | bytes 705024 | tf_op jit(solution)/shard_map/all_gather | solution.py:95
  50.5 0.2 fusion.60
  50.7 0.2 convolution_convert_fusion
  50.9 20.3 %all_gather.22 = f32[256,384]{1,0:T(8,128)S(1)} all-gather(f32[16,384]{1,0:T(8,128)S(1)} %copy-done), channel_id=1, replica_groups=mesh['grp'=8,'dom'=16] {'dom'}, dimensions={0}, use_global_device_ids=true | all-gather | bytes 417792 | tf_op jit(solution)/shard_map/all_gather | solution.py:79
  71.2 0.2 select_reduce_fusion
  72.0 0.4 fusion.39
  72.4 1.9 %broadcast_multiply_fusion = bf16[32,48,6,4,4,4]{1,0,5,4,3,2:T(8,128)(2,1)S(1)} fusion(f32[48,6,4,4,4]{0,4,3,2,1:T(4,128)S(1)} %broadcast_multiply_fusion.2, f32[32,6,4,4,4]{0,4,3,2,1:T(4,128)S(1)} %bitcast.40), kind=kLoop, calls=%fused_computation.11 | loop fusion | flops 1179648 | bytes 1302528 | tf_op jit(solution)/shard_map/mul | solution.py:19
  74.4 0.3 fusion.37
  74.7 1.3 reverse_select_fusion.2
  76.0 1.5 reverse_select_fusion.1
  77.5 1.1 fusion
  78.6 8.9 %fusion.17 = bf16[32,48,48]{2,1,0:T(8,128)(2,1)} fusion(bf16[32,384,384]{2,1,0:T(8,128)(2,1)} %param.13, bf16[32,48,384]{1,0,2:T(8,128)(2,1)S(1)} %bitcast.37, f32[48,384]{1,0:T(8,128)S(1)} %mul.191, f32[32,384]{1,0:T(8,128)S(1)} %fusion.37), kind=kOutput, calls=%fused_computation.23 | convolution fusion | flops 511451136 | bytes 10887168 | tf_op jit(solution)/shard_map/rci,rdi->rcd/dot_general | solution.py:47
  87.5 1.4 convert_element_type.111
  88.9 0.7 maximum_bitcast_fusion
  89.7 2.8 %convert_element_type.105 = f32[256,2304]{1,0:T(8,128)} convert(bf16[256,2304]{1,0:T(8,128)(2,1)} %all-gather.7.cloned.1.call-done) | non-fusion elementwise | flops 589824 | bytes 3538944 | tf_op jit(solution)/shard_map/convert_element_type | solution.py:139
  92.5 54.4 %all-gather.9.cloned.1.call-done = bf16[16,57,2304]{2,1,0:T(8,128)(2,1)} async-done(((bf16[1,57,2304]{2,1,0:T(8,128)(2,1)}), bf16[16,57,2304]{2,1,0:T(8,128)(2,1)}) %all-gather.9.cloned.1.call-update) | async-done | bytes 4202512 | tf_op jit(solution)/shard_map/all_gather | solution.py:127
  146.9 0.8 slice_convert_fusion
  147.9 0.2 slice.30
  148.2 2.2 %slice-done = bf16[16,56,2304]{2,1,0:T(8,128)(2,1)S(1)} async-done(((bf16[16,57,2304]{2,1,0:T(8,128)(2,1)}), bf16[16,56,2304]{2,1,0:T(8,128)(2,1)S(1)}, s32[]{:S(2)}) %slice-start) | async-done | bytes 4128792 | tf_op jit(solution)/shard_map/slice | solution.py:129
  150.4 6.0 %fusion.4 = f32[768,2304]{1,0:T(8,128)} fusion(bf16[896,2304]{1,0:T(8,128)(2,1)S(1)} %bitcast.39, s32[896]{0:T(1024)S(1)} %select_n.198), kind=kOutput, calls=%fused_computation.13 | convolution fusion | flops 3171581952 | bytes 11210240 | tf_op jit(solution)/shard_map/dot_general | solution.py:138
  156.3 8.6 %reshape.527 = f32[256,6912]{1,0:T(8,128)} reshape(f32[768,2304]{1,0:T(8,128)} %fusion.4) | data formatting | bytes 14155776 | tf_op jit(solution)/shard_map/reshape | solution.py:140
  (68 shorter events, 2.6 us)
Async XLA Ops:
  7.2 6.0 %copy-start = (f32[16,384]{1,0:T(8,128)S(1)}, f32[16,384]{1,0:T(8,128)}, u32[]{:S(2)}) copy-start(f32[16,384]{1,0:T(8,128)} %param.15) | copy-start | bytes 73732
  7.2 82.5 %all-gather.7.cloned.1.call-start = ((), (), s32[]{:S(2)}) async-start(), calls=%async_computation | async-start | bytes 1253376 | tf_op jit(solution)/shard_map/all_gather | solution.py:84
  7.7 20.4 %copy-start.1 = (s32[16]{0:T(128)S(1)}, s32[16]{0:T(128)}, u32[]{:S(2)}) copy-start(s32[16]{0:T(128)} %param.17) | copy-start | bytes 196
  7.7 20.7 %copy-start.3 = (s32[16]{0:T(128)S(1)}, s32[16]{0:T(128)}, u32[]{:S(2)}) copy-start(s32[16]{0:T(128)} %param.19) | copy-start | bytes 196
  7.7 20.7 %copy-start.5 = (s32[16,1]{0,1:T(1,128)S(1)}, s32[16,1]{0,1:T(1,128)}, u32[]{:S(2)}) copy-start(s32[16,1]{0,1:T(1,128)} %param.21) | copy-start | bytes 196
  7.8 20.8 %copy-start.4 = (s32[16]{0:T(128)S(1)}, s32[16]{0:T(128)}, u32[]{:S(2)}) copy-start(s32[16]{0:T(128)} %param.23) | copy-start | bytes 196
  12.9 134.0 %all-gather.9.cloned.1.call-start = ((), (), s32[]{:S(2)}) async-start(), calls=%async_computation.1 | async-start | bytes 5013504 | tf_op jit(solution)/shard_map/all_gather | solution.py:127
  31.8 39.7 %copy-start.6 = (s32[32]{0:T(128)S(1)}, s32[32]{0:T(128)}, u32[]{:S(2)}) copy-start(s32[32]{0:T(128)} %param.22) | copy-start | bytes 388
  31.8 39.7 %copy-start.7 = (s32[32,1]{0,1:T(1,128)S(1)}, s32[32,1]{0,1:T(1,128)}, u32[]{:S(2)}) copy-start(s32[32,1]{0,1:T(1,128)} %param.20) | copy-start | bytes 388
  31.8 40.2 %copy-start.2 = (s32[32]{0:T(128)S(1)}, s32[32]{0:T(128)}, u32[]{:S(2)}) copy-start(s32[32]{0:T(128)} %param.16) | copy-start | bytes 388
  36.6 37.8 %copy-start.8 = (s32[32]{0:T(128)S(1)}, s32[32]{0:T(128)}, u32[]{:S(2)}) copy-start(s32[32]{0:T(128)} %param.18) | copy-start | bytes 388
  148.2 2.2 %slice-start = ((bf16[16,57,2304]{2,1,0:T(8,128)(2,1)}), bf16[16,56,2304]{2,1,0:T(8,128)(2,1)S(1)}, s32[]{:S(2)}) async-start(bf16[16,57,2304]{2,1,0:T(8,128)(2,1)} %all-gather.9.cloned.1.call-done), calls=%async_computation.2 | async-start | bytes 8257536 | tf_op jit(solution)/shard_map/slice | solution.py:129
Sparse Core Ops, SparseCore 0:
  13.0 44.4 all-gather.6
  89.8 57.1 all-gather.8
where the time goes:
time: 172 us
  waiting for transfers between devices  54.5 us (32%)
  blocking collectives  48.4 us (28%)
  matrix products  24.8 us (14%)
  local copies, waits for them, and re-layouts  15.2 us (9%)
  between operations  14.4 us (8%)
  other arithmetic  14.3 us (8%)
    all_gather x1, waiting for transfers between devices, per_device(): face_all = lax.all_gather(face_packet, 'dom', axis=0)  54.4 us
    all_gather x1, blocking collectives, per_device(): metric_dom = lax.all_gather(metric, 'dom', axis=0, tiled=True)  20.3 us
    dot_general x3, matrix products, coarse_terms(): jnp.einsum('rci,rdi->rcd', row_side, products, preferred_element_type=jnp...  17.4 us
    all_gather x1, blocking collectives, per_device(): metric_grp = lax.all_gather(metric, 'grp', axis=0, tiled=True)  14.6 us
    all_gather x1, blocking collectives, per_device(): cross_got = lax.all_gather(cross_packet, 'grp', axis=0)  13.5 us
    reshape x1, local copies, waits for them, and re-layouts, per_device(): coarse_face = face.reshape(group_width * elem_count, 3 * square)  8.64 us
    dot_general x1, matrix products, per_device(): face = jnp.dot(onehot, contrib, preferred_element_type=jnp.float32)  5.97 us
  transfers between devices with their start and end apart: 2, of which 1 were waited for; matrix products, arithmetic and copies ran while one was open for 18% of the time, Pallas kernels for 0%

commit v1 on v0

--- a/solution.py
+++ b/solution.py
@@ -4,6 +4,24 @@
 from jax.sharding import PartitionSpec as P
 
 CROSS_CAP = 3
+
+
+def collect(shard, axis, dim):
+    ways, here, turn = (lax.axis_size(axis), lax.axis_index(axis), shard.shape[dim])
+    shape = [n * ways if d == dim else n for d, n in enumerate(shard.shape)]
+    full = lax.dynamic_update_slice_in_dim(
+        jnp.zeros(shape, shard.dtype), shard, here * turn, axis=dim
+    )
+    going_up = going_down = shard
+    for far in range(1, ways // 2 + 1):
+        going_up = lax.ppermute(going_up, axis, [(d, (d + 1) % ways) for d in range(ways)])
+        full = lax.dynamic_update_slice_in_dim(full, going_up, (here - far) % ways * turn, axis=dim)
+        if 2 * far < ways:
+            going_down = lax.ppermute(going_down, axis, [(d, (d - 1) % ways) for d in range(ways)])
+            full = lax.dynamic_update_slice_in_dim(
+                full, going_down, (here + far) % ways * turn, axis=dim
+            )
+    return full
 
 
 def corner_table(var_count):
@@ -76,7 +94,7 @@
     my_grp = lax.axis_index("grp")
     inner_count = face_in.shape[0]
     cross_count = face_cross.shape[0]
-    metric_dom = lax.all_gather(metric, "dom", axis=0, tiled=True)
+    metric_dom = collect(metric, "dom", 0)
     metric_grp = lax.all_gather(metric, "grp", axis=0, tiled=True)
     diag_side = plain_restrictor(metric)
     diag_c = coarse_terms(diag_side, one_sided(diag_blocks, diag_side))

time: 172 us -> 205 us (1.19)
  starting transfers between devices: 0.08 us -> 35.8 us
  blocking collectives: 48.4 us -> 28.8 us
  local copies, waits for them, and re-layouts: 15.2 us -> 25.1 us
  waiting for transfers between devices: 54.5 us -> 59.1 us
    ppermute x0 -> x15, starting transfers between devices: none -> 35.7 us  [the longest x7 33.5 us: collect(): lax.ppermute(going_down, axis, [(d, (d - 1) % ways) for d in range(ways)])]
    all_gather x1 -> x0, blocking collectives: 20.3 us -> none  [per_device(): metric_dom = lax.all_gather(metric, 'dom', axis=0, tiled=True)]
    dynamic_update_slice x0 -> x16, local copies, waits for them, and re-layouts: none -> 9.15 us  [the longest x8 4.87 us: collect(): lax.dynamic_update_slice_in_dim(full, going_up, (here - far) % ways * tur...]
    ppermute x0 -> x15, waiting for transfers between devices: none -> 4.81 us  [the longest x8 4.79 us: collect(): lax.ppermute(going_up, axis, [(d, (d + 1) % ways) for d in range(ways)])]
  transfers between devices with their start and end apart: 2 -> 17, of which waited for: 1 -> 2; matrix products, arithmetic and copies ran while one was open for 18% -> 23% of each run, Pallas kernels for 0% -> 0%
where the time goes in v1:
time: 205 us
  waiting for transfers between devices  59.1 us (29%)
  starting transfers between devices  35.8 us (17%)
  blocking collectives  28.8 us (14%)
  matrix products  26.5 us (13%)
  local copies, waits for them, and re-layouts  25.1 us (12%)
  between operations  14.9 us (7%)
  other arithmetic  14.6 us (7%)
    all_gather x1, waiting for transfers between devices, per_device(): face_all = lax.all_gather(face_packet, 'dom', axis=0)  54.3 us
    ppermute x7, starting transfers between devices, collect(): lax.ppermute(going_down, axis, [(d, (d - 1) % ways) for d in range(ways)])  33.5 us
    dot_general x3, matrix products, coarse_terms(): jnp.einsum('rci,rdi->rcd', row_side, products, preferred_element_type=jnp...  17.4 us
    all_gather x1, blocking collectives, per_device(): metric_grp = lax.all_gather(metric, 'grp', axis=0, tiled=True)  15.2 us
    all_gather x1, blocking collectives, per_device(): cross_got = lax.all_gather(cross_packet, 'grp', axis=0)  13.7 us
    reshape x1, local copies, waits for them, and re-layouts, per_device(): coarse_face = face.reshape(group_width * elem_count, 3 * square)  8.64 us
    dot_general x1, matrix products, per_device(): face = jnp.dot(onehot, contrib, preferred_element_type=jnp.float32)  5.98 us
    dynamic_update_slice x8, local copies, waits for them, and re-layouts, collect(): lax.dynamic_update_slice_in_dim(full, going_up, (here - far) % ways * tur...  4.87 us
  transfers between devices with their start and end apart: 17, of which 2 were waited for; matrix products, arithmetic and copies ran while one was open for 23% of the time, Pallas kernels for 0%

profile of v1, /device:TPU:1, one launch (start us, length us, event | category | flops | bytes accessed | tf_op | source)
XLA Modules:
  0.0 204.9 jit_solution(15847165574928504634)
XLA Ops:
  7.2 2.1 %collective-permute-start = (f32[16,384]{1,0:T(8,128)}, f32[16,384]{1,0:T(8,128)S(1)}, u32[]{:S(2)}, u32[]{:S(2)}) collective-permute-start(f32[16,384]{1,0:T(8,128)} %param.15), channel_id=1, source_target_pairs={{0,1},{1,2},{2,3},{3,4},{4,5},{5,6},{6,7},{7,8},{8,9},{9,10},{10,1... | collective-permute-start | bytes 73736 | tf_op jit(solution)/shard_map/ppermute | solution.py:17
  9.3 4.8 %collective-permute-start.1 = (f32[16,384]{1,0:T(8,128)}, f32[16,384]{1,0:T(8,128)S(1)}, u32[]{:S(2)}, u32[]{:S(2)}) collective-permute-start(f32[16,384]{1,0:T(8,128)} %param.15), channel_id=1, source_target_pairs={{0,15},{1,0},{2,1},{3,2},{4,3},{5,4},{6,5},{7,6},{8,7},{9,8},{10,9... | collective-permute-start | bytes 73736 | tf_op jit(solution)/shard_map/ppermute | solution.py:20
  14.7 4.3 %fusion.26 = bf16[16,48,48]{2,1,0:T(8,128)(2,1)S(1)} fusion(bf16[16,384,384]{2,1,0:T(8,128)(2,1)} %param.12, f32[48,384]{1,0:T(8,128)S(1)} %mul.239, f32[16,384]{1,0:T(8,128)} %param.15), kind=kOutput, calls=%fused_computation.30 | convolution fusion | flops 256315392 | bytes 4890624 | tf_op jit(solution)/shard_map/rci,rdi->rcd/dot_general | solution.py:65
  19.0 0.9 convert_element_type.104
  20.1 15.2 %all_gather.19 = f32[128,384]{1,0:T(8,128)} all-gather(f32[16,384]{1,0:T(8,128)S(1)} %copy-done.1), channel_id=1, replica_groups=mesh['grp'=8,'dom'=16] {'grp'}, dimensions={0}, use_global_device_ids=true | all-gather | bytes 221184 | tf_op jit(solution)/shard_map/all_gather | solution.py:98
  36.0 1.0 broadcast_multiply_fusion.1
  37.6 0.7 reverse_select_fusion.4
  39.2 4.3 %fusion.27 = bf16[16,48,48]{2,1,0:T(8,128)(2,1)S(1)} fusion(bf16[16,384,384]{2,1,0:T(8,128)(2,1)} %param.14, bf16[16,48,384]{1,0,2:T(8,128)(2,1)S(1)} %bitcast.38, f32[16,384]{1,0:T(8,128)S(1)} %fusion.42, f32[48,384]{1,0:T(8,128)S(1)} %mul.239), kind=kOutput, calls=%fused_computation.31 | convolution fusion | flops 255725568 | bytes 5480448 | tf_op jit(solution)/shard_map/rci,rdi->rcd/dot_general | solution.py:65
  44.0 13.7 %all-gather.2 = bf16[8,17,2304]{2,1,0:T(8,128)(2,1)S(1)} all-gather(bf16[1,17,2304]{2,1,0:T(8,128)(2,1)S(1)} %maximum_bitcast_fusion.1), channel_id=2, replica_groups=mesh['grp'=8,'dom'=16] {'grp'}, dimensions={0}, use_global_device_ids=true | all-gather | bytes 705024 | tf_op jit(solution)/shard_map/all_gather | solution.py:113
  58.3 0.9 convolution_convert_fusion
  59.5 1.9 broadcast_multiply_fusion
  61.9 0.7 copy-done
  62.7 1.3 reverse_select_fusion.2
  64.0 1.5 reverse_select_fusion.1
  65.5 1.5 fusion
  67.9 4.8 %collective-permute-start.3 = (f32[16,384]{1,0:T(8,128)S(1)}, f32[16,384]{1,0:T(8,128)S(1)}, u32[]{:S(2)}, u32[]{:S(2)}) collective-permute-start(f32[16,384]{1,0:T(8,128)S(1)} %collective-permute-done.1), channel_id=1, source_target_pairs={{0,15},{1,0},{2,1},{3,2},{4,3},{5,4},{6,5},{7,6},{8,7},{9,8},{10,9... | collective-permute-start | bytes 73736 | tf_op jit(solution)/shard_map/ppermute | solution.py:20
  73.9 4.8 %collective-permute-start.5 = (f32[16,384]{1,0:T(8,128)S(1)}, f32[16,384]{1,0:T(8,128)S(1)}, u32[]{:S(2)}, u32[]{:S(2)}) collective-permute-start(f32[16,384]{1,0:T(8,128)S(1)} %collective-permute-done.3), channel_id=1, source_target_pairs={{0,15},{1,0},{2,1},{3,2},{4,3},{5,4},{6,5},{7,6},{8,7},{9,8},{10,9... | collective-permute-start | bytes 73736 | tf_op jit(solution)/shard_map/ppermute | solution.py:20
  79.9 4.8 %collective-permute-start.7 = (f32[16,384]{1,0:T(8,128)S(1)}, f32[16,384]{1,0:T(8,128)S(1)}, u32[]{:S(2)}, u32[]{:S(2)}) collective-permute-start(f32[16,384]{1,0:T(8,128)S(1)} %collective-permute-done.5), channel_id=1, source_target_pairs={{0,15},{1,0},{2,1},{3,2},{4,3},{5,4},{6,5},{7,6},{8,7},{9,8},{10,9... | collective-permute-start | bytes 73736 | tf_op jit(solution)/shard_map/ppermute | solution.py:20
  85.9 4.8 %collective-permute-start.9 = (f32[16,384]{1,0:T(8,128)S(1)}, f32[16,384]{1,0:T(8,128)S(1)}, u32[]{:S(2)}, u32[]{:S(2)}) collective-permute-start(f32[16,384]{1,0:T(8,128)S(1)} %collective-permute-done.7), channel_id=1, source_target_pairs={{0,15},{1,0},{2,1},{3,2},{4,3},{5,4},{6,5},{7,6},{8,7},{9,8},{10,9... | collective-permute-start | bytes 73736 | tf_op jit(solution)/shard_map/ppermute | solution.py:20
  92.0 4.8 %collective-permute-start.11 = (f32[16,384]{1,0:T(8,128)S(1)}, f32[16,384]{1,0:T(8,128)S(1)}, u32[]{:S(2)}, u32[]{:S(2)}) collective-permute-start(f32[16,384]{1,0:T(8,128)S(1)} %collective-permute-done.9), channel_id=1, source_target_pairs={{0,15},{1,0},{2,1},{3,2},{4,3},{5,4},{6,5},{7,6},{8,7},{9,8},{10,9... | collective-permute-start | bytes 73736 | tf_op jit(solution)/shard_map/ppermute | solution.py:20
  98.0 4.8 %collective-permute-start.13 = (f32[16,384]{1,0:T(8,128)S(1)}, f32[16,384]{1,0:T(8,128)S(1)}, u32[]{:S(2)}, u32[]{:S(2)}) collective-permute-start(f32[16,384]{1,0:T(8,128)S(1)} %collective-permute-done.11), channel_id=1, source_target_pairs={{0,15},{1,0},{2,1},{3,2},{4,3},{5,4},{6,5},{7,6},{8,7},{9,8},{10,9... | collective-permute-start | bytes 73736 | tf_op jit(solution)/shard_map/ppermute | solution.py:20
  105.2 4.8 %collective-permute-done.14 = f32[16,384]{1,0:T(8,128)S(1)} collective-permute-done((f32[16,384]{1,0:T(8,128)S(1)}, f32[16,384]{1,0:T(8,128)S(1)}, u32[]{:S(2)}, u32[]{:S(2)}) %collective-permute-start.14) | collective-permute-done | bytes 24608 | tf_op jit(solution)/shard_map/ppermute | solution.py:17
  110.6 1.3 fusion.37
  111.8 8.9 %fusion.17 = bf16[32,48,48]{2,1,0:T(8,128)(2,1)} fusion(bf16[32,384,384]{2,1,0:T(8,128)(2,1)} %param.13, bf16[32,48,384]{1,0,2:T(8,128)(2,1)S(1)} %bitcast.37, f32[48,384]{1,0:T(8,128)S(1)} %mul.239, f32[32,384]{1,0:T(8,128)S(1)} %fusion.37), kind=kOutput, calls=%fused_computation.23 | convolution fusion | flops 511451136 | bytes 10887168 | tf_op jit(solution)/shard_map/rci,rdi->rcd/dot_general | solution.py:65
  120.7 1.4 convert_element_type.111
  122.1 0.7 maximum_bitcast_fusion
  122.9 2.8 %convert_element_type.105 = f32[256,2304]{1,0:T(8,128)} convert(bf16[256,2304]{1,0:T(8,128)(2,1)} %all-gather.7.cloned.1.call-done) | non-fusion elementwise | flops 589824 | bytes 3538944 | tf_op jit(solution)/shard_map/convert_element_type | solution.py:157
  125.7 54.3 %all-gather.9.cloned.1.call-done = bf16[16,57,2304]{2,1,0:T(8,128)(2,1)} async-done(((bf16[1,57,2304]{2,1,0:T(8,128)(2,1)}), bf16[16,57,2304]{2,1,0:T(8,128)(2,1)}) %all-gather.9.cloned.1.call-update) | async-done | bytes 4202512 | tf_op jit(solution)/shard_map/all_gather | solution.py:145
  180.0 0.8 slice_convert_fusion
  181.2 2.2 %slice-done = bf16[16,56,2304]{2,1,0:T(8,128)(2,1)S(1)} async-done(((bf16[16,57,2304]{2,1,0:T(8,128)(2,1)}), bf16[16,56,2304]{2,1,0:T(8,128)(2,1)S(1)}, s32[]{:S(2)}) %slice-start) | async-done | bytes 4128792 | tf_op jit(solution)/shard_map/slice | solution.py:147
  183.4 6.0 %fusion.4 = f32[768,2304]{1,0:T(8,128)} fusion(bf16[896,2304]{1,0:T(8,128)(2,1)S(1)} %bitcast.39, s32[896]{0:T(1024)S(1)} %select_n.339), kind=kOutput, calls=%fused_computation.13 | convolution fusion | flops 3171581952 | bytes 11210240 | tf_op jit(solution)/shard_map/dot_general | solution.py:156
  189.4 8.6 %reshape.527 = f32[256,6912]{1,0:T(8,128)} reshape(f32[768,2304]{1,0:T(8,128)} %fusion.4) | data formatting | bytes 14155776 | tf_op jit(solution)/shard_map/reshape | solution.py:158
  (120 shorter events, 14.9 us)
Async XLA Ops:
  7.2 12.9 %copy-start.1 = (f32[16,384]{1,0:T(8,128)S(1)}, f32[16,384]{1,0:T(8,128)}, u32[]{:S(2)}) copy-start(f32[16,384]{1,0:T(8,128)} %param.15) | copy-start | bytes 73732
  7.2 115.7 %all-gather.7.cloned.1.call-start = ((), (), s32[]{:S(2)}) async-start(), calls=%async_computation | async-start | bytes 1253376 | tf_op jit(solution)/shard_map/all_gather | solution.py:102
  7.2 60.6 %collective-permute-start = (f32[16,384]{1,0:T(8,128)}, f32[16,384]{1,0:T(8,128)S(1)}, u32[]{:S(2)}, u32[]{:S(2)}) collective-permute-start(f32[16,384]{1,0:T(8,128)} %param.15), channel_id=1, source_target_pairs={{0,1},{1,2},{2,3},{3,4},{4,5},{5,6},{6,7},{7,8},{8,9},{9,10},{10,1... | collective-permute-start | bytes 73736 | tf_op jit(solution)/shard_map/ppermute | solution.py:17
  9.3 58.6 %collective-permute-start.1 = (f32[16,384]{1,0:T(8,128)}, f32[16,384]{1,0:T(8,128)S(1)}, u32[]{:S(2)}, u32[]{:S(2)}) collective-permute-start(f32[16,384]{1,0:T(8,128)} %param.15), channel_id=1, source_target_pairs={{0,15},{1,0},{2,1},{3,2},{4,3},{5,4},{6,5},{7,6},{8,7},{9,8},{10,9... | collective-permute-start | bytes 73736 | tf_op jit(solution)/shard_map/ppermute | solution.py:20
  14.6 20.9 %copy-start.4 = (s32[16]{0:T(128)S(1)}, s32[16]{0:T(128)}, u32[]{:S(2)}) copy-start(s32[16]{0:T(128)} %param.17) | copy-start | bytes 196
  14.6 21.3 %copy-start.6 = (s32[16]{0:T(128)S(1)}, s32[16]{0:T(128)}, u32[]{:S(2)}) copy-start(s32[16]{0:T(128)} %param.19) | copy-start | bytes 196
  14.6 21.3 %copy-start.8 = (s32[16,1]{0,1:T(1,128)S(1)}, s32[16,1]{0,1:T(1,128)}, u32[]{:S(2)}) copy-start(s32[16,1]{0,1:T(1,128)} %param.21) | copy-start | bytes 196
  14.7 21.3 %copy-start.7 = (s32[16]{0:T(128)S(1)}, s32[16]{0:T(128)}, u32[]{:S(2)}) copy-start(s32[16]{0:T(128)} %param.23) | copy-start | bytes 196
  19.8 160.1 %all-gather.9.cloned.1.call-start = ((), (), s32[]{:S(2)}) async-start(), calls=%async_computation.1 | async-start | bytes 5013504 | tf_op jit(solution)/shard_map/all_gather | solution.py:145
  37.6 1.3 copy-start.2
  39.2 20.0 %copy-start.5 = (s32[32]{0:T(128)S(1)}, s32[32]{0:T(128)}, u32[]{:S(2)}) copy-start(s32[32]{0:T(128)} %param.16) | copy-start | bytes 388
  43.5 18.0 %copy-start.9 = (s32[32]{0:T(128)S(1)}, s32[32]{0:T(128)}, u32[]{:S(2)}) copy-start(s32[32]{0:T(128)} %param.18) | copy-start | bytes 388
  43.7 18.2 %copy-start.10 = (s32[32]{0:T(128)S(1)}, s32[32]{0:T(128)}, u32[]{:S(2)}) copy-start(s32[32]{0:T(128)} %param.22) | copy-start | bytes 388
  43.7 18.2 %copy-start.11 = (s32[32,1]{0,1:T(1,128)S(1)}, s32[32,1]{0,1:T(1,128)}, u32[]{:S(2)}) copy-start(s32[32,1]{0,1:T(1,128)} %param.20) | copy-start | bytes 388
  61.9 0.7 copy-start
  65.5 2.2 %copy-start.3 = (bf16[8,3,2304]{2,1,0:T(4,128)(2,1)S(1)}, bf16[8,3,2304]{2,1,0:T(4,128)(2,1)}, u32[]{:S(2)}) copy-start(bf16[8,3,2304]{2,1,0:T(4,128)(2,1)} %convolution_convert_fusion) | copy-start | bytes 331780
  67.8 6.1 %collective-permute-start.2 = (f32[16,384]{1,0:T(8,128)S(1)}, f32[16,384]{1,0:T(8,128)S(1)}, u32[]{:S(2)}, u32[]{:S(2)}) collective-permute-start(f32[16,384]{1,0:T(8,128)S(1)} %collective-permute-done), channel_id=1, source_target_pairs={{0,1},{1,2},{2,3},{3,4},{4,5},{5,6},{6,7},{7,8},{8,9},{9,10},{10,1... | collective-permute-start | bytes 73736 | tf_op jit(solution)/shard_map/ppermute | solution.py:17
  67.9 6.0 %collective-permute-start.3 = (f32[16,384]{1,0:T(8,128)S(1)}, f32[16,384]{1,0:T(8,128)S(1)}, u32[]{:S(2)}, u32[]{:S(2)}) collective-permute-start(f32[16,384]{1,0:T(8,128)S(1)} %collective-permute-done.1), channel_id=1, source_target_pairs={{0,15},{1,0},{2,1},{3,2},{4,3},{5,4},{6,5},{7,6},{8,7},{9,8},{10,9... | collective-permute-start | bytes 73736 | tf_op jit(solution)/shard_map/ppermute | solution.py:20
  73.9 6.0 %collective-permute-start.4 = (f32[16,384]{1,0:T(8,128)S(1)}, f32[16,384]{1,0:T(8,128)S(1)}, u32[]{:S(2)}, u32[]{:S(2)}) collective-permute-start(f32[16,384]{1,0:T(8,128)S(1)} %collective-permute-done.2), channel_id=1, source_target_pairs={{0,1},{1,2},{2,3},{3,4},{4,5},{5,6},{6,7},{7,8},{8,9},{9,10},{10,1... | collective-permute-start | bytes 73736 | tf_op jit(solution)/shard_map/ppermute | solution.py:17
  73.9 6.0 %collective-permute-start.5 = (f32[16,384]{1,0:T(8,128)S(1)}, f32[16,384]{1,0:T(8,128)S(1)}, u32[]{:S(2)}, u32[]{:S(2)}) collective-permute-start(f32[16,384]{1,0:T(8,128)S(1)} %collective-permute-done.3), channel_id=1, source_target_pairs={{0,15},{1,0},{2,1},{3,2},{4,3},{5,4},{6,5},{7,6},{8,7},{9,8},{10,9... | collective-permute-start | bytes 73736 | tf_op jit(solution)/shard_map/ppermute | solution.py:20
  79.9 6.0 %collective-permute-start.6 = (f32[16,384]{1,0:T(8,128)S(1)}, f32[16,384]{1,0:T(8,128)S(1)}, u32[]{:S(2)}, u32[]{:S(2)}) collective-permute-start(f32[16,384]{1,0:T(8,128)S(1)} %collective-permute-done.4), channel_id=1, source_target_pairs={{0,1},{1,2},{2,3},{3,4},{4,5},{5,6},{6,7},{7,8},{8,9},{9,10},{10,1... | collective-permute-start | bytes 73736 | tf_op jit(solution)/shard_map/ppermute | solution.py:17
  79.9 6.0 %collective-permute-start.7 = (f32[16,384]{1,0:T(8,128)S(1)}, f32[16,384]{1,0:T(8,128)S(1)}, u32[]{:S(2)}, u32[]{:S(2)}) collective-permute-start(f32[16,384]{1,0:T(8,128)S(1)} %collective-permute-done.5), channel_id=1, source_target_pairs={{0,15},{1,0},{2,1},{3,2},{4,3},{5,4},{6,5},{7,6},{8,7},{9,8},{10,9... | collective-permute-start | bytes 73736 | tf_op jit(solution)/shard_map/ppermute | solution.py:20
  85.9 6.0 %collective-permute-start.8 = (f32[16,384]{1,0:T(8,128)S(1)}, f32[16,384]{1,0:T(8,128)S(1)}, u32[]{:S(2)}, u32[]{:S(2)}) collective-permute-start(f32[16,384]{1,0:T(8,128)S(1)} %collective-permute-done.6), channel_id=1, source_target_pairs={{0,1},{1,2},{2,3},{3,4},{4,5},{5,6},{6,7},{7,8},{8,9},{9,10},{10,1... | collective-permute-start | bytes 73736 | tf_op jit(solution)/shard_map/ppermute | solution.py:17
  85.9 6.0 %collective-permute-start.9 = (f32[16,384]{1,0:T(8,128)S(1)}, f32[16,384]{1,0:T(8,128)S(1)}, u32[]{:S(2)}, u32[]{:S(2)}) collective-permute-start(f32[16,384]{1,0:T(8,128)S(1)} %collective-permute-done.7), channel_id=1, source_target_pairs={{0,15},{1,0},{2,1},{3,2},{4,3},{5,4},{6,5},{7,6},{8,7},{9,8},{10,9... | collective-permute-start | bytes 73736 | tf_op jit(solution)/shard_map/ppermute | solution.py:20
  91.9 6.0 %collective-permute-start.10 = (f32[16,384]{1,0:T(8,128)S(1)}, f32[16,384]{1,0:T(8,128)S(1)}, u32[]{:S(2)}, u32[]{:S(2)}) collective-permute-start(f32[16,384]{1,0:T(8,128)S(1)} %collective-permute-done.8), channel_id=1, source_target_pairs={{0,1},{1,2},{2,3},{3,4},{4,5},{5,6},{6,7},{7,8},{8,9},{9,10},{10,1... | collective-permute-start | bytes 73736 | tf_op jit(solution)/shard_map/ppermute | solution.py:17
  92.0 6.0 %collective-permute-start.11 = (f32[16,384]{1,0:T(8,128)S(1)}, f32[16,384]{1,0:T(8,128)S(1)}, u32[]{:S(2)}, u32[]{:S(2)}) collective-permute-start(f32[16,384]{1,0:T(8,128)S(1)} %collective-permute-done.9), channel_id=1, source_target_pairs={{0,15},{1,0},{2,1},{3,2},{4,3},{5,4},{6,5},{7,6},{8,7},{9,8},{10,9... | collective-permute-start | bytes 73736 | tf_op jit(solution)/shard_map/ppermute | solution.py:20
  98.0 6.0 %collective-permute-start.12 = (f32[16,384]{1,0:T(8,128)S(1)}, f32[16,384]{1,0:T(8,128)S(1)}, u32[]{:S(2)}, u32[]{:S(2)}) collective-permute-start(f32[16,384]{1,0:T(8,128)S(1)} %collective-permute-done.10), channel_id=1, source_target_pairs={{0,1},{1,2},{2,3},{3,4},{4,5},{5,6},{6,7},{7,8},{8,9},{9,10},{10,1... | collective-permute-start | bytes 73736 | tf_op jit(solution)/shard_map/ppermute | solution.py:17
  98.0 6.6 %collective-permute-start.13 = (f32[16,384]{1,0:T(8,128)S(1)}, f32[16,384]{1,0:T(8,128)S(1)}, u32[]{:S(2)}, u32[]{:S(2)}) collective-permute-start(f32[16,384]{1,0:T(8,128)S(1)} %collective-permute-done.11), channel_id=1, source_target_pairs={{0,15},{1,0},{2,1},{3,2},{4,3},{5,4},{6,5},{7,6},{8,7},{9,8},{10,9... | collective-permute-start | bytes 73736 | tf_op jit(solution)/shard_map/ppermute | solution.py:20
  104.0 6.0 %collective-permute-start.14 = (f32[16,384]{1,0:T(8,128)S(1)}, f32[16,384]{1,0:T(8,128)S(1)}, u32[]{:S(2)}, u32[]{:S(2)}) collective-permute-start(f32[16,384]{1,0:T(8,128)S(1)} %collective-permute-done.12), channel_id=1, source_target_pairs={{0,1},{1,2},{2,3},{3,4},{4,5},{5,6},{6,7},{7,8},{8,9},{9,10},{10,1... | collective-permute-start | bytes 73736 | tf_op jit(solution)/shard_map/ppermute | solution.py:17
  181.2 2.2 %slice-start = ((bf16[16,57,2304]{2,1,0:T(8,128)(2,1)}), bf16[16,56,2304]{2,1,0:T(8,128)(2,1)S(1)}, s32[]{:S(2)}) async-start(bf16[16,57,2304]{2,1,0:T(8,128)(2,1)} %all-gather.9.cloned.1.call-done), calls=%async_computation.2 | async-start | bytes 8257536 | tf_op jit(solution)/shard_map/slice | solution.py:147
Sparse Core Ops, SparseCore 0:
  20.0 39.7 all-gather.6
  123.0 56.9 all-gather.8
